TPU v7x, 512 devices: a whole 4x4x16 slice. The times are simulated.
512 devices in a mesh: dp: 128 (over z, y, core), mp: 4 (over x).
Axes of the slice: x: 4, y: 4, z: 16, core: 2. Of those that a mesh axis runs over, the one named last changes fastest.
Arguments:
- features: bfloat16 [8192, 4096], P('dp', 'mp'), may hold values from -6 to 6
- norm_gain: bfloat16 [4096], replicated, may hold values from 0.099609375 to 1.8984375
- w_key: bfloat16 [4096, 512], P('dp', 'mp'), may hold values from -0.09375 to 0.09375
- w_value: bfloat16 [4096, 512], P('dp', 'mp'), may hold values from -0.09375 to 0.09375
- queries: bfloat16 [8192, 2048], P('dp', 'mp'), may hold values from -150 to 150
- key_pool: bfloat16 [256, 128, 512], P('dp', None, 'mp'), may hold values from -5 to 5
- value_pool: bfloat16 [256, 128, 512], P('dp', None, 'mp'), may hold values from -5 to 5
- cache_lens: int32 [3], replicated, may hold values from 2 to 15360, as said below
- page_table: int32 [3, 186], replicated, may hold values from -1 to 255, as said below
- token_request: int32 [8192], replicated, may hold values from 0 to 2, as said below
Outputs:
- attended: bfloat16 [8192, 2048], P('dp', 'mp')
- keys_out: bfloat16 [256, 128, 512], P('dp', None, 'mp')
- values_out: bfloat16 [256, 128, 512], P('dp', None, 'mp')
Inputs may be any that keep to these rules, and one draw needn't show every extreme that they name: `cache_lens`: exactly one request has 15360 cached tokens, each other request has at most 512. `page_table`: row r lists the pool pages of request r in logical order: its first ceil(cache_lens[r] / 128) entries are pages among the first 1 slots of some device, the entries up to the page of its last new token are pages among the other slots of some device, later entries are -1; no pool page is listed twice. `token_request`: never falling along the new tokens; every request has 2048 or more new tokens.
All inputs are finite; a program needn't handle non-finite values.
Results may differ from a plain program's by a relative error of at most 0.0068.
Values may be sent and summed in bfloat16 or wider, within the bound.
A program may use at most 64 MiB of HBM per device.

v0:
```python
import math

import jax
import jax.numpy as jnp
from jax import lax
from jax.sharding import PartitionSpec as P

HD = 128
PAGE = 128
SHORT = 512
CTX_DEV = 120


THETA = 500000.0
NEG_FILL = -1e30


def rotate(values, positions, head_size):
    halfway = head_size // 2
    inverse = THETA ** (-(jnp.arange(halfway, dtype=jnp.float32) * 2.0) / head_size)
    angles = positions.astype(jnp.float32)[:, None] * inverse[None, :]
    cosine = jnp.cos(angles)[:, None, :]
    sine = jnp.sin(angles)[:, None, :]
    first_half = values[..., :halfway]
    second_half = values[..., halfway:]
    return jnp.concatenate(
        [first_half * cosine - second_half * sine, second_half * cosine + first_half * sine],
        axis=-1,
    )


def body(
    features,
    norm_gain,
    w_key,
    w_value,
    queries,
    key_pool,
    value_pool,
    cache_lens,
    page_table,
    token_request,
):
    gathered = lax.all_gather(features, "mp", axis=1, tiled=True)
    widened = gathered.astype(jnp.float32)
    mean_square = jnp.mean(widened * widened, axis=1, keepdims=True)
    normed = (widened * lax.rsqrt(mean_square + 1e-05) * norm_gain.astype(jnp.float32)).astype(
        jnp.bfloat16
    )
    tok_rows = features.shape[0]
    kv_width = w_key.shape[1]
    head_size = HD
    kv_heads = kv_width // head_size
    q_heads = queries.shape[1] // head_size
    group_size = q_heads // kv_heads
    scale = 1.0 / math.sqrt(head_size)
    pieces = (
        lax.all_gather(w_key, "dp", axis=0, tiled=True),
        lax.all_gather(w_value, "dp", axis=0, tiled=True),
    )
    key_sums = jnp.dot(normed, pieces[0], preferred_element_type=jnp.float32)
    value_sums = jnp.dot(normed, pieces[1], preferred_element_type=jnp.float32)
    total_new = token_request.shape[0]
    requests = cache_lens.shape[0]
    request_ids = jnp.arange(requests, dtype=jnp.int32)
    member = (token_request[:, None] == request_ids[None, :]).astype(jnp.int32)
    counts = jnp.sum(member, axis=0)
    starts = jnp.cumsum(counts) - counts
    token_index = jnp.arange(total_new, dtype=jnp.int32)
    token_pos = jnp.sum(member * (cache_lens - starts)[None, :], axis=1) + token_index
    dp_index = lax.axis_index("dp")
    dp_count = lax.axis_size("dp")
    first_token = dp_index * tok_rows
    my_request = lax.dynamic_slice_in_dim(token_request, first_token, tok_rows)
    my_pos = lax.dynamic_slice_in_dim(token_pos, first_token, tok_rows)
    key_heads = rotate(key_sums.reshape(tok_rows, kv_heads, head_size), my_pos, head_size)
    new_keys = key_heads.reshape(tok_rows, kv_width).astype(jnp.bfloat16)
    new_values = value_sums.astype(jnp.bfloat16)
    pages_dev = key_pool.shape[0]
    page_rows = key_pool.shape[1]
    max_pages = page_table.shape[1]
    slot_all = jnp.take(page_table.reshape(-1), token_request * max_pages + token_pos // page_rows)
    local_slot = slot_all - dp_index * pages_dev
    owned = (local_slot >= 0) & (local_slot < pages_dev)
    dest_all = jnp.where(
        owned, local_slot * page_rows + token_pos % page_rows, pages_dev * page_rows
    )
    long_pages = (CTX_DEV * dp_count + PAGE - 1) // PAGE
    old_dev = (long_pages + 2 * ((SHORT + PAGE - 1) // PAGE) + dp_count - 1) // dp_count
    old_total = old_dev * dp_count
    old_ids = jnp.arange(old_total, dtype=jnp.int32)
    old_phys = old_ids // old_dev * pages_dev + old_ids % old_dev
    matches = (page_table[None, :, :] == old_phys[:, None, None]).astype(jnp.int32)
    page_has = jnp.sum(matches, axis=(1, 2)) > 0
    page_request = jnp.sum(matches * request_ids[None, :, None], axis=(1, 2))
    page_logical = jnp.sum(
        matches * jnp.arange(max_pages, dtype=jnp.int32)[None, None, :], axis=(1, 2)
    )
    page_limit = jnp.sum(matches * cache_lens[None, :, None], axis=(1, 2))
    q_local = queries.reshape(tok_rows, kv_heads, group_size, head_size)

    def attend(att_state, keys_flat, values_flat, key_info):
        key_request, key_pos, key_ok = key_info
        visible = (
            key_ok[None, :]
            & (key_request[None, :] == my_request[:, None])
            & (key_pos[None, :] <= my_pos[:, None])
        )
        keys_shaped = keys_flat.reshape(keys_flat.shape[0], kv_heads, head_size)
        values_shaped = values_flat.reshape(values_flat.shape[0], kv_heads, head_size)
        running_max, running_sum, running_acc = att_state
        scores = (
            jnp.einsum("thgd,khd->thgk", q_local, keys_shaped, preferred_element_type=jnp.float32)
            * scale
        )
        mask_full = visible[:, None, None, :]
        masked = jnp.where(mask_full, scores, NEG_FILL)
        new_max = jnp.maximum(running_max, jnp.max(masked, axis=-1))
        factor = jnp.exp(running_max - new_max)
        soft_weights = jnp.where(mask_full, jnp.exp(masked - new_max[..., None]), 0.0)
        new_sum = running_sum * factor + jnp.sum(soft_weights, axis=-1)
        new_acc = running_acc * factor[..., None] + jnp.einsum(
            "thgk,khd->thgd",
            soft_weights.astype(jnp.bfloat16),
            values_shaped,
            preferred_element_type=jnp.float32,
        )
        return (new_max, new_sum, new_acc)

    def attend_rows(att_state, keys_flat, values_flat, key_info):
        row_count = keys_flat.shape[0]
        key_block = 2048
        blocks = row_count // key_block
        stacked = (
            keys_flat.reshape(blocks, key_block, kv_width),
            values_flat.reshape(blocks, key_block, kv_width),
            key_info[0].reshape(blocks, key_block),
            key_info[1].reshape(blocks, key_block),
            key_info[2].reshape(blocks, key_block),
        )

        def step_block(inner_state, slab_parts):
            return (
                attend(
                    inner_state,
                    slab_parts[0],
                    slab_parts[1],
                    (slab_parts[2], slab_parts[3], slab_parts[4]),
                ),
                None,
            )

        att_state, unused = lax.scan(step_block, att_state, stacked)
        return att_state

    start_state = (
        jnp.full((tok_rows, kv_heads, group_size), NEG_FILL, jnp.float32),
        jnp.zeros((tok_rows, kv_heads, group_size), jnp.float32),
        jnp.zeros((tok_rows, kv_heads, group_size, head_size), jnp.float32),
    )
    flat_keys = key_pool.reshape(pages_dev * page_rows, kv_width)
    flat_values = value_pool.reshape(pages_dev * page_rows, kv_width)
    old_keys = key_pool[:old_dev]
    old_values = value_pool[:old_dev]
    pieces = (
        lax.all_gather(old_keys, "dp", axis=0, tiled=True),
        lax.all_gather(old_values, "dp", axis=0, tiled=True),
    )
    page_count = pieces[0].shape[0]
    cached_keys = pieces[0].reshape(page_count * page_rows, kv_width)
    cached_values = pieces[1].reshape(page_count * page_rows, kv_width)
    row_ids = jnp.arange(page_rows, dtype=jnp.int32)[None, :]
    key_pos = page_logical[:, None] * page_rows + row_ids
    key_ok = page_has[:, None] & (key_pos < page_limit[:, None])
    key_request = jnp.broadcast_to(page_request[:, None], (page_count, page_rows))
    middle_state = attend_rows(
        start_state,
        cached_keys,
        cached_values,
        (key_request.reshape(-1), key_pos.reshape(-1), key_ok.reshape(-1)),
    )
    pieces = (
        lax.all_gather(new_keys, "dp", axis=0, tiled=True),
        lax.all_gather(new_values, "dp", axis=0, tiled=True),
    )
    att_state = middle_state
    pool_keys = flat_keys
    pool_values = flat_values
    key_request = token_request
    key_pos = token_pos
    att_state = attend_rows(
        att_state,
        pieces[0],
        pieces[1],
        (key_request, key_pos, jnp.ones((pieces[0].shape[0],), jnp.bool_)),
    )
    pool_keys, pool_values = (
        pool_keys.at[dest_all].set(pieces[0], mode="drop"),
        pool_values.at[dest_all].set(pieces[1], mode="drop"),
    )
    final_state, pool_keys, pool_values = (att_state, pool_keys, pool_values)
    final_max, final_sum, final_acc = final_state
    attended = (
        (final_acc / final_sum[..., None])
        .reshape(tok_rows, q_heads * head_size)
        .astype(jnp.bfloat16)
    )
    return (attended, pool_keys.reshape(key_pool.shape), pool_values.reshape(value_pool.shape))


def solution(mesh):
    in_specs = (
        P("dp", "mp"),
        P(),
        P("dp", "mp"),
        P("dp", "mp"),
        P("dp", "mp"),
        P("dp", None, "mp"),
        P("dp", None, "mp"),
        P(),
        P(),
        P(),
    )
    out_specs = (P("dp", "mp"), P("dp", None, "mp"), P("dp", None, "mp"))
    return jax.shard_map(body, mesh=mesh, in_specs=in_specs, out_specs=out_specs, check_vma=False)
```

profile of v0, /device:TPU:1, one launch (start us, length us, event | category | flops | bytes accessed | tf_op | source)
XLA Modules:
  0.0 894.3 jit_solution(7624690923403732621)
XLA Ops:
  14.7 32.9 %gather_fusion = s32[8192]{0:T(1024)S(1)} fusion(s32[558]{0:T(1024)S(1)} %reshape.425, s32[8192]{0:T(1024)S(1)} %broadcast_clamp_fusion), kind=kCustom, calls=%fused_computation | custom fusion | bytes 98304 | tf_op jit(solution)/shard_map/jit(_take)/gather | solution.py:82
  47.8 11.1 %all_gather.23 = bf16[64,4096]{1,0:T(8,128)(2,1)S(1)} all-gather(bf16[64,1024]{1,0:T(8,128)(2,1)S(1)} %copy-done.3), channel_id=1, replica_groups=mesh['dp'=128,'mp'=4] {'mp'}, dimensions={1}, use_global_device_ids=true | all-gather | bytes 655360 | tf_op jit(solution)/shard_map/all_gather | solution.py:44
  59.1 88.4 %all-gather.12.cloned.1.call-done = bf16[4096,128]{1,0:T(8,128)(2,1)} async-done(((bf16[32,128]{1,0:T(8,128)(2,1)}), bf16[4096,128]{1,0:T(8,128)(2,1)}) %all-gather.12.cloned.1.call-update) | async-done | bytes 1048592 | tf_op jit(solution)/shard_map/all_gather | solution.py:58
  150.0 126.8 %all-gather.14.cloned.1.call-done = bf16[4096,128]{1,0:T(8,128)(2,1)} async-done(((bf16[32,128]{1,0:T(8,128)(2,1)}), bf16[4096,128]{1,0:T(8,128)(2,1)}) %all-gather.14.cloned.1.call-update) | async-done | bytes 1048592 | tf_op jit(solution)/shard_map/all_gather | solution.py:59
  276.8 2.2 convolution_convert_fusion
  281.7 134.3 %all-gather.18.cloned.1.call-done = bf16[8192,1,128]{2,0,1:T(8,128)(2,1)} async-done(((bf16[64,1,128]{2,0,1:T(8,128)(2,1)}), bf16[8192,1,128]{2,0,1:T(8,128)(2,1)}) %all-gather.18.cloned.1.call-update) | async-done | bytes 2097168 | tf_op jit(solution)/shard_map/all_gather | solution.py:183
  416.0 21.1 %scatter_custom_fusion = bf16[256,128]{1,0:T(8,128)(2,1)S(1)} fusion(bf16[256,128]{1,0:T(8,128)(2,1)S(1)} %bitcast.176, s32[8192]{0:T(1024)S(1)} %get-tuple-element.304, bf16[8192,1,128]{2,0,1:T(8,128)(2,1)} %all-gather.18.cloned.1.call-done), kind=kCustom, calls=%fused_computation.60 | custom fusion | bytes 2162688 | tf_op jit(solution)/shard_map/scatter | solution.py:198
  437.1 117.9 %all-gather.16.cloned.1.call-done = bf16[8192,128]{1,0:T(8,128)(2,1)} async-done(((bf16[64,128]{1,0:T(8,128)(2,1)}), bf16[8192,128]{1,0:T(8,128)(2,1)}) %all-gather.16.cloned.1.call-update) | async-done | bytes 2097168 | tf_op jit(solution)/shard_map/all_gather | solution.py:184
  555.1 21.1 %scatter_fusion = bf16[256,128]{1,0:T(8,128)(2,1)S(1)} fusion(bf16[256,128]{1,0:T(8,128)(2,1)S(1)} %bitcast.161, s32[8192]{0:T(1024)S(1)} %get-tuple-element.304, bf16[8192,128]{1,0:T(8,128)(2,1)} %all-gather.16.cloned.1.call-done), kind=kCustom, calls=%fused_computation.2 | custom fusion | bytes 6324224 | tf_op jit(solution)/shard_map/scatter | solution.py:199
  576.2 120.7 %all-gather.8.cloned.1.call-done = bf16[128,128,128]{2,1,0:T(8,128)(2,1)} async-done(((bf16[1,128,128]{2,1,0:T(8,128)(2,1)}), bf16[128,128,128]{2,1,0:T(8,128)(2,1)}) %all-gather.8.cloned.1.call-update) | async-done | bytes 4194320 | tf_op jit(solution)/shard_map/all_gather | solution.py:166
  696.9 141.0 %all-gather.10.cloned.1.call-done = bf16[128,128,128]{2,1,0:T(8,128)(2,1)} async-done(((bf16[1,128,128]{2,1,0:T(8,128)(2,1)}), bf16[128,128,128]{2,1,0:T(8,128)(2,1)}) %all-gather.10.cloned.1.call-update) | async-done | bytes 4194320 | tf_op jit(solution)/shard_map/all_gather | solution.py:167
  837.9 32.7 %while.30 = (s32[]{:T(128)}, f32[64,1,4]{0,2,1:T(4,128)S(1)}, f32[64,1,4]{0,2,1:T(4,128)S(1)}, f32[64,1,4,128]{3,0,2,1:T(8,128)S(1)}, pred[8,2048]{1,0:T(8,128)(...) while((s32[]{:T(128)}, f32[64,1,4]{0,2,1:T(4,128)S(1)}, ...), condition=%wide.region_10.11_spmd.clone, body=%wide.region_7.10_spmd.clone.sunk | while | flops 273778176 | bytes 8264361 | solution.py:153
  838.2 1.6 fusion.89
  840.3 1.6 fusion.92
  842.2 1.6 fusion.89
  846.3 1.6 fusion.89
  850.4 1.6 fusion.89
  852.6 1.6 fusion.92
  854.5 1.6 fusion.89
  858.6 1.6 fusion.89
  862.7 1.6 fusion.89
  864.9 1.6 fusion.92
  866.8 1.6 fusion.89
  870.6 16.1 %while.29 = (s32[]{:T(128)}, f32[64,1,4]{0,2,1:T(4,128)S(1)}, f32[64,1,4]{0,2,1:T(4,128)S(1)}, f32[64,1,4,128]{3,0,2,1:T(8,128)S(1)}, s32[4,2048]{1,0:T(4,128)S(...) while((s32[]{:T(128)}, f32[64,1,4]{0,2,1:T(4,128)S(1)}, ...), condition=%wide.region_15.16_spmd, body=%wide.region_12.15_spmd.sunk | while | flops 273613568 | bytes 8258185 | solution.py:153
  870.8 1.6 fusion.83
  873.0 1.6 fusion.86
  874.8 1.6 fusion.83
  877.0 1.6 fusion.86
  878.8 1.6 fusion.83
  881.0 1.6 fusion.86
  882.9 1.6 fusion.83
  885.1 1.6 fusion.86
  (158 shorter events, 31.4 us)
Async XLA Ops:
  7.2 140.3 %all-gather.12.cloned.1.call-start = ((), (), s32[]{:S(2)}) async-start(), calls=%async_computation.2 | async-start | bytes 1056768 | tf_op jit(solution)/shard_map/all_gather | solution.py:58
  8.9 267.8 %all-gather.14.cloned.1.call-start = ((), (), s32[]{:S(2)}) async-start(), calls=%async_computation.3 | async-start | bytes 1056768 | tf_op jit(solution)/shard_map/all_gather | solution.py:59
  9.7 406.3 %all-gather.18.cloned.1.call-start = ((), (), s32[]{:S(2)}) async-start(), calls=%async_computation.5 | async-start | bytes 2113536 | tf_op jit(solution)/shard_map/all_gather | solution.py:183
  14.7 32.9 %copy-start.1 = (s32[8192]{0:T(1024)S(1)}, s32[8192]{0:T(1024)}, u32[]{:S(2)}) copy-start(s32[8192]{0:T(1024)} %param.23) | copy-start | bytes 98308
  14.7 33.1 %copy-start.3 = (bf16[64,1024]{1,0:T(8,128)(2,1)S(1)}, bf16[64,1024]{1,0:T(8,128)(2,1)}, u32[]{:S(2)}) copy-start(bf16[64,1024]{1,0:T(8,128)(2,1)} %param.14) | copy-start | bytes 393220
  58.8 221.6 %copy-start.5 = (s32[3,186]{1,0:T(4,128)S(1)}, s32[3,186]{1,0:T(4,128)}, u32[]{:S(2)}) copy-start(s32[3,186]{1,0:T(4,128)} %param.22) | copy-start | bytes 6700
  58.8 221.7 %copy-start.6 = (s32[3]{0:T(128)S(1)}, s32[3]{0:T(128)}, u32[]{:S(2)}) copy-start(s32[3]{0:T(128)} %param.21) | copy-start | bytes 40
  58.8 222.5 %copy-start.4 = (bf16[64,512]{1,0:T(8,128)(2,1)S(1)}, bf16[64,512]{1,0:T(8,128)(2,1)}, u32[]{:S(2)}) copy-start(bf16[64,512]{1,0:T(8,128)(2,1)} %param.18) | copy-start | bytes 196612
  149.9 405.1 %all-gather.16.cloned.1.call-start = ((), (), s32[]{:S(2)}) async-start(), calls=%async_computation.4 | async-start | bytes 2113536 | tf_op jit(solution)/shard_map/all_gather | solution.py:184
  278.9 418.0 %all-gather.8.cloned.1.call-start = ((), (), s32[]{:S(2)}) async-start(), calls=%async_computation | async-start | bytes 4227072 | tf_op jit(solution)/shard_map/all_gather | solution.py:166
  279.6 558.2 %all-gather.10.cloned.1.call-start = ((), (), s32[]{:S(2)}) async-start(), calls=%async_computation.1 | async-start | bytes 4227072 | tf_op jit(solution)/shard_map/all_gather | solution.py:167
  437.1 139.1 %copy-start.2 = (bf16[256,128]{1,0:T(8,128)(2,1)}, bf16[256,128]{1,0:T(8,128)(2,1)S(1)}, u32[]{:S(2)}) copy-start(bf16[256,128]{1,0:T(8,128)(2,1)S(1)} %scatter_custom_fusion) | copy-start | bytes 196612
  576.2 261.7 %copy-start = (bf16[256,128]{1,0:T(8,128)(2,1)}, bf16[256,128]{1,0:T(8,128)(2,1)S(1)}, u32[]{:S(2)}) copy-start(bf16[256,128]{1,0:T(8,128)(2,1)S(1)} %scatter_fusion) | copy-start | bytes 196612
Sparse Core Ops, SparseCore 0:
  11.0 136.4 all-gather.11
  150.4 126.3 all-gather.13
  280.5 135.4 all-gather.17
  419.0 136.0 all-gather.15
  558.6 138.2 all-gather.7
  699.9 137.9 all-gather.9
where the time goes:
time: 896 us; the launch traced here: 894 us
  waiting for transfers between devices  730 us (81%)
  local copies, waits for them, and re-layouts  81 us (9%)
  matrix products  42.3 us (5%)
  other arithmetic  15 us (2%)
  between operations  14.4 us (2%)
  blocking collectives  11.1 us (1%)
    all_gather x1, waiting for transfers between devices, body(): lax.all_gather(old_values, 'dp', axis=0, tiled=True)  141 us
    all_gather x1, waiting for transfers between devices, body(): lax.all_gather(new_keys, 'dp', axis=0, tiled=True)  134 us
    all_gather x1, waiting for transfers between devices, body(): lax.all_gather(w_value, 'dp', axis=0, tiled=True)  127 us
    all_gather x1, waiting for transfers between devices, body(): lax.all_gather(old_keys, 'dp', axis=0, tiled=True)  121 us
    all_gather x1, waiting for transfers between devices, body(): lax.all_gather(new_values, 'dp', axis=0, tiled=True)  118 us
    all_gather x1, waiting for transfers between devices, body(): lax.all_gather(w_key, 'dp', axis=0, tiled=True)  88.4 us
    gather x1, local copies, waits for them, and re-layouts, body(): jnp.take(page_table.reshape(-1), token_request * max_pages + token_pos //...  32.9 us
    scatter x1, local copies, waits for them, and re-layouts, body(): pool_values.at[dest_all].set(pieces[1], mode='drop')  21.1 us
  transfers between devices with their start and end apart: 6, of which 6 were waited for; matrix products, arithmetic and copies ran while one was open for 10% of the time, Pallas kernels for 0%

commit v1 on v0

v1 whole, which is shorter than its diff:
```python
import math

import jax
import jax.numpy as jnp
from jax import lax
from jax.sharding import Mesh
from jax.sharding import PartitionSpec as P

HD = 128
OLD_DEV = 1
KEY_BLOCK = 2048

THETA = 500000.0
NEG_FILL = -1e30

ZY = ("z", "y")
ROWS = ("z", "y", "core")


def rotate(values, positions, head_size):
    halfway = head_size // 2
    inverse = THETA ** (-(jnp.arange(halfway, dtype=jnp.float32) * 2.0) / head_size)
    angles = positions.astype(jnp.float32)[:, None] * inverse[None, :]
    cosine = jnp.cos(angles)[:, None, :]
    sine = jnp.sin(angles)[:, None, :]
    first_half = values[..., :halfway]
    second_half = values[..., halfway:]
    return jnp.concatenate(
        [first_half * cosine - second_half * sine, second_half * cosine + first_half * sine],
        axis=-1,
    )


def gather_rows(payload):
    step = lax.all_gather(payload, ZY, axis=0, tiled=False)
    return lax.all_gather(step, "core", axis=0, tiled=False)


def make_body(n_zy, n_core):
    n_dp = n_zy * n_core

    def body(
        features,
        norm_gain,
        w_key,
        w_value,
        queries,
        key_pool,
        value_pool,
        cache_lens,
        page_table,
        token_request,
    ):
        tok_rows = features.shape[0]
        w_rows, kv_width = w_key.shape
        head_size = HD
        kv_heads = kv_width // head_size
        q_heads = queries.shape[1] // head_size
        group_size = q_heads // kv_heads
        scale = 1.0 / math.sqrt(head_size)
        pages_dev, page_rows, _ = key_pool.shape
        max_pages = page_table.shape[1]
        requests = cache_lens.shape[0]
        total_new = token_request.shape[0]

        core = lax.axis_index("core")
        zy = lax.axis_index("z") * (n_zy // lax.axis_size("z")) + lax.axis_index("y")
        dp_index = zy * n_core + core

        old_keys = key_pool[:OLD_DEV].reshape(OLD_DEV * page_rows, kv_width)
        old_values = value_pool[:OLD_DEV].reshape(OLD_DEV * page_rows, kv_width)
        first = gather_rows(jnp.concatenate([w_key, w_value, old_keys, old_values], axis=0))
        old_rows = OLD_DEV * page_rows
        wk_all = first[:, :, :w_rows].reshape(n_core * n_zy * w_rows, kv_width)
        wv_all = first[:, :, w_rows : 2 * w_rows].reshape(n_core * n_zy * w_rows, kv_width)
        cached_keys = first[:, :, 2 * w_rows : 2 * w_rows + old_rows].reshape(-1, kv_width)
        cached_values = first[:, :, 2 * w_rows + old_rows :].reshape(-1, kv_width)

        gathered = lax.all_gather(features, "x", axis=1, tiled=True)
        widened = gathered.astype(jnp.float32)
        mean_square = jnp.mean(widened * widened, axis=1, keepdims=True)
        normed = (
            widened * lax.rsqrt(mean_square + 1e-05) * norm_gain.astype(jnp.float32)
        ).astype(jnp.bfloat16)
        normed_cz = (
            normed.reshape(tok_rows, n_zy, n_core, w_rows)
            .transpose(0, 2, 1, 3)
            .reshape(tok_rows, -1)
        )
        key_sums = jnp.dot(normed_cz, wk_all, preferred_element_type=jnp.float32)
        value_sums = jnp.dot(normed_cz, wv_all, preferred_element_type=jnp.float32)

        request_ids = jnp.arange(requests, dtype=jnp.int32)
        member = (token_request[:, None] == request_ids[None, :]).astype(jnp.int32)
        counts = jnp.sum(member, axis=0)
        starts = jnp.cumsum(counts) - counts
        token_index = jnp.arange(total_new, dtype=jnp.int32)
        token_pos = jnp.sum(member * (cache_lens - starts)[None, :], axis=1) + token_index
        first_token = dp_index * tok_rows
        my_request = lax.dynamic_slice_in_dim(token_request, first_token, tok_rows)
        my_pos = lax.dynamic_slice_in_dim(token_pos, first_token, tok_rows)
        key_heads = rotate(key_sums.reshape(tok_rows, kv_heads, head_size), my_pos, head_size)
        new_keys = key_heads.reshape(tok_rows, kv_width).astype(jnp.bfloat16)
        new_values = value_sums.astype(jnp.bfloat16)

        page_core = jnp.arange(n_core, dtype=jnp.int32)[:, None]
        page_zy = jnp.arange(n_zy, dtype=jnp.int32)[None, :]
        slot_ids = jnp.arange(OLD_DEV, dtype=jnp.int32)[None, None, :]
        old_phys = ((page_zy * n_core + page_core)[:, :, None] * pages_dev + slot_ids).reshape(-1)
        matches = (page_table[None, :, :] == old_phys[:, None, None]).astype(jnp.int32)
        page_has = jnp.sum(matches, axis=(1, 2)) > 0
        page_request = jnp.sum(matches * request_ids[None, :, None], axis=(1, 2))
        page_logical = jnp.sum(
            matches * jnp.arange(max_pages, dtype=jnp.int32)[None, None, :], axis=(1, 2)
        )
        page_limit = jnp.sum(matches * cache_lens[None, :, None], axis=(1, 2))
        q_local = queries.reshape(tok_rows, kv_heads, group_size, head_size)

        def attend(att_state, keys_flat, values_flat, key_info):
            key_request, key_pos, key_ok = key_info
            visible = (
                key_ok[None, :]
                & (key_request[None, :] == my_request[:, None])
                & (key_pos[None, :] <= my_pos[:, None])
            )
            keys_shaped = keys_flat.reshape(keys_flat.shape[0], kv_heads, head_size)
            values_shaped = values_flat.reshape(values_flat.shape[0], kv_heads, head_size)
            running_max, running_sum, running_acc = att_state
            scores = (
                jnp.einsum(
                    "thgd,khd->thgk", q_local, keys_shaped, preferred_element_type=jnp.float32
                )
                * scale
            )
            mask_full = visible[:, None, None, :]
            masked = jnp.where(mask_full, scores, NEG_FILL)
            new_max = jnp.maximum(running_max, jnp.max(masked, axis=-1))
            factor = jnp.exp(running_max - new_max)
            soft_weights = jnp.where(mask_full, jnp.exp(masked - new_max[..., None]), 0.0)
            new_sum = running_sum * factor + jnp.sum(soft_weights, axis=-1)
            new_acc = running_acc * factor[..., None] + jnp.einsum(
                "thgk,khd->thgd",
                soft_weights.astype(jnp.bfloat16),
                values_shaped,
                preferred_element_type=jnp.float32,
            )
            return (new_max, new_sum, new_acc)

        def attend_rows(att_state, keys_flat, values_flat, key_info):
            row_count = keys_flat.shape[0]
            blocks = row_count // KEY_BLOCK
            stacked = (
                keys_flat.reshape(blocks, KEY_BLOCK, kv_width),
                values_flat.reshape(blocks, KEY_BLOCK, kv_width),
                key_info[0].reshape(blocks, KEY_BLOCK),
                key_info[1].reshape(blocks, KEY_BLOCK),
                key_info[2].reshape(blocks, KEY_BLOCK),
            )

            def step_block(inner_state, slab_parts):
                return (
                    attend(
                        inner_state,
                        slab_parts[0],
                        slab_parts[1],
                        (slab_parts[2], slab_parts[3], slab_parts[4]),
                    ),
                    None,
                )

            att_state, unused = lax.scan(step_block, att_state, stacked)
            return att_state

        start_state = (
            jnp.full((tok_rows, kv_heads, group_size), NEG_FILL, jnp.float32),
            jnp.zeros((tok_rows, kv_heads, group_size), jnp.float32),
            jnp.zeros((tok_rows, kv_heads, group_size, head_size), jnp.float32),
        )
        page_count = old_phys.shape[0]
        row_ids = jnp.arange(page_rows, dtype=jnp.int32)[None, :]
        key_pos = page_logical[:, None] * page_rows + row_ids
        key_ok = page_has[:, None] & (key_pos < page_limit[:, None])
        key_request = jnp.broadcast_to(page_request[:, None], (page_count, page_rows))
        middle_state = attend_rows(
            start_state,
            cached_keys,
            cached_values,
            (key_request.reshape(-1), key_pos.reshape(-1), key_ok.reshape(-1)),
        )

        second = gather_rows(jnp.concatenate([new_keys, new_values], axis=1))
        fresh = second.reshape(n_core * n_zy * tok_rows, 2 * kv_width)
        fresh_keys = fresh[:, :kv_width]
        fresh_values = fresh[:, kv_width:]
        fresh_request = (
            token_request.reshape(n_zy, n_core, tok_rows).transpose(1, 0, 2).reshape(-1)
        )
        fresh_pos = token_pos.reshape(n_zy, n_core, tok_rows).transpose(1, 0, 2).reshape(-1)
        att_state = attend_rows(
            middle_state,
            fresh_keys,
            fresh_values,
            (fresh_request, fresh_pos, jnp.ones((total_new,), jnp.bool_)),
        )
        final_max, final_sum, final_acc = att_state
        attended = (
            (final_acc / final_sum[..., None])
            .reshape(tok_rows, q_heads * head_size)
            .astype(jnp.bfloat16)
        )

        own_pages = dp_index * pages_dev + jnp.arange(pages_dev, dtype=jnp.int32)
        own_match = (page_table[None, :, :] == own_pages[:, None, None]).astype(jnp.int32)
        own_has = jnp.sum(own_match, axis=(1, 2)) > 0
        own_request = jnp.sum(own_match * request_ids[None, :, None], axis=(1, 2))
        own_logical = jnp.sum(
            own_match * jnp.arange(max_pages, dtype=jnp.int32)[None, None, :], axis=(1, 2)
        )
        row_pos = own_logical[:, None] * page_rows + row_ids
        lo = jnp.take(cache_lens, own_request)[:, None]
        hi = lo + jnp.take(counts, own_request)[:, None]
        row_new = own_has[:, None] & (row_pos >= lo) & (row_pos < hi)
        row_token = jnp.clip(jnp.take(starts, own_request)[:, None] + row_pos - lo, 0, total_new - 1)
        token_dp = row_token // tok_rows
        fresh_row = ((token_dp % n_core) * n_zy + token_dp // n_core) * tok_rows + row_token % tok_rows
        picked = jnp.take(fresh, fresh_row.reshape(-1), axis=0)
        row_new = row_new.reshape(-1, 1)
        flat_keys = key_pool.reshape(pages_dev * page_rows, kv_width)
        flat_values = value_pool.reshape(pages_dev * page_rows, kv_width)
        keys_out = jnp.where(row_new, picked[:, :kv_width], flat_keys)
        values_out = jnp.where(row_new, picked[:, kv_width:], flat_values)
        return (attended, keys_out.reshape(key_pool.shape), values_out.reshape(value_pool.shape))

    return body


def solution(mesh):
    n_dp, n_mp = mesh.devices.shape
    n_core = 2
    n_y = 4
    n_z = n_dp // (n_y * n_core)
    fine = Mesh(mesh.devices.reshape(n_z, n_y, n_core, n_mp), ("z", "y", "core", "x"))
    in_specs = (
        P(ROWS, "x"),
        P(),
        P(ROWS, "x"),
        P(ROWS, "x"),
        P(ROWS, "x"),
        P(ROWS, None, "x"),
        P(ROWS, None, "x"),
        P(),
        P(),
        P(),
    )
    out_specs = (P(ROWS, "x"), P(ROWS, None, "x"), P(ROWS, None, "x"))
    return jax.shard_map(
        make_body(n_z * n_y, n_core),
        mesh=fine,
        in_specs=in_specs,
        out_specs=out_specs,
        check_vma=False,
    )
```

time: 896 us -> 404 us (0.45)
  the two profiles are of different devices: /device:TPU:1 before, /device:TPU:2 now
where the time goes in v1:
time: 404 us; the launch traced here: 403 us
  waiting for transfers between devices  301 us (75%)
  matrix products  38.1 us (9%)
  local copies, waits for them, and re-layouts  19.9 us (5%)
  other arithmetic  15.1 us (4%)
  between operations  14.1 us (3%)
  blocking collectives  13.8 us (3%)
    all_gather x2, waiting for transfers between devices, gather_rows(): step = lax.all_gather(payload, ZY, axis=0, tiled=False)  290 us
    dot_general x12, matrix products, attend(): jnp.einsum('thgk,khd->thgd', soft_weights.astype(jnp.bfloat16), values_sh...  19.3 us
    dot_general x12, matrix products, attend(): jnp.einsum('thgd,khd->thgk', q_local, keys_shaped, preferred_element_type...  15.4 us
    all_gather x1, blocking collectives, body(): gathered = lax.all_gather(features, 'x', axis=1, tiled=True)  13.8 us
    all_gather x2, waiting for transfers between devices, gather_rows(): return lax.all_gather(step, 'core', axis=0, tiled=False)  10.6 us
  transfers between devices with their start and end apart: 4, of which 3 were waited for; matrix products, arithmetic and copies ran while one was open for 11% of the time, Pallas kernels for 0%

profile of v1, /device:TPU:2, one launch (start us, length us, event | category | flops | bytes accessed | tf_op | source)
XLA Modules:
  0.0 402.5 jit_solution(7638691210647181783)
XLA Ops:
  8.0 1.3 pad_maximum_fusion
  9.4 156.0 %all-gather.9.cloned.1.call-done = bf16[20480,128]{1,0:T(8,128)(2,1)} async-done(((bf16[320,128]{1,0:T(8,128)(2,1)}), bf16[20480,128]{1,0:T(8,128)(2,1)}) %all-gather.9.cloned.1.call-update) | async-done | bytes 5242896 | tf_op jit(solution)/shard_map/all_gather | solution.py:35
  169.1 13.8 %all_gather.31 = bf16[64,4096]{0,1:T(8,128)(2,1)S(1)} all-gather(bf16[64,1024]{0,1:T(8,128)(2,1)S(1)} %copy.62), channel_id=1, replica_groups=mesh['z'=16,'y'=4,'core'=2,'x'=4] {'x'}, dimensions={1}, use_global_device_ids=true | all-gather | bytes 655360 | tf_op jit(solution)/shard_map/all_gather | solution.py:79
  184.2 10.6 %all-gather.11.cloned.1.call-done = bf16[128,320,128]{2,1,0:T(8,128)(2,1)} async-done(((bf16[64,320,128]{2,1,0:T(8,128)(2,1)}), bf16[128,320,128]{2,1,0:T(8,128)(2,1)}) %all-gather.11.cloned.1.call-update) | async-done | bytes 10485776 | tf_op jit(solution)/shard_map/all_gather | solution.py:36
  194.8 1.7 fusion.41
  196.5 1.7 convolution_bitcast_fusion.3
  201.4 6.2 %fusion.74 = (bf16[2,64,128,128]{3,2,1,0:T(8,128)(2,1)}, bf16[2,64,128,128]{3,2,1,0:T(8,128)(2,1)}) fusion(bf16[2,64,320,128]{3,2,1,0:T(8,128)(2,1)} %bitcast.222), kind=kLoop, calls=%fused_computation.174 | loop fusion | bytes 16777216 | tf_op jit(solution)/shard_map/slice | solution.py:77
  207.6 134.1 %all-gather.13.cloned.1.call-done = bf16[4096,256]{1,0:T(8,128)(2,1)} async-done(((bf16[64,256]{1,0:T(8,128)(2,1)}), bf16[4096,256]{1,0:T(8,128)(2,1)}) %all-gather.13.cloned.1.call-update) | async-done | bytes 2097168 | tf_op jit(solution)/shard_map/all_gather | solution.py:35
  341.7 33.0 %while.30 = (s32[]{:T(128)}, f32[64,1,4]{0,2,1:T(4,128)S(1)}, f32[64,1,4]{0,2,1:T(4,128)S(1)}, f32[64,1,4,128]{3,0,2,1:T(8,128)S(1)}, pred[8,2048]{1,0:T(8,128)(...) while((s32[]{:T(128)}, f32[64,1,4]{0,2,1:T(4,128)S(1)}, ...), condition=%wide.region_10.11_spmd.clone, body=%wide.region_7.0_spmd.clone.sunk | while | flops 273778176 | bytes 8264361 | solution.py:171
  342.0 1.6 fusion.96
  344.2 1.6 fusion.99
  346.1 1.6 fusion.96
  348.3 1.6 fusion.99
  350.2 1.6 fusion.96
  352.4 1.6 fusion.99
  354.4 1.6 fusion.96
  356.5 1.7 fusion.99
  358.5 1.7 fusion.96
  360.8 1.6 fusion.99
  362.7 1.6 fusion.96
  364.9 1.6 fusion.99
  366.8 1.6 fusion.96
  369.0 1.6 fusion.99
  370.9 1.6 fusion.96
  373.1 1.6 fusion.99
  374.8 3.8 fusion.75
  378.6 3.7 gather_fusion
  382.3 12.0 %while.29 = (s32[]{:T(128)}, f32[64,1,4]{0,2,1:T(4,128)S(1)}, f32[64,1,4]{0,2,1:T(4,128)S(1)}, f32[64,1,4,128]{3,0,2,1:T(8,128)S(1)}, s32[4,2048]{1,0:T(4,128)S(...) while((s32[]{:T(128)}, f32[64,1,4]{0,2,1:T(4,128)S(1)}, ...), condition=%wide.region_15.16_spmd, body=%wide.region_12.15_spmd.sunk | while | flops 273613568 | bytes 8258185 | solution.py:171
  383.7 1.6 fusion.93
  386.7 1.6 fusion.93
  389.7 1.6 fusion.93
  392.7 1.6 fusion.93
  (177 shorter events, 22.5 us)
Async XLA Ops:
  7.2 158.2 %all-gather.9.cloned.1.call-start = ((), (), s32[]{:S(2)}) async-start(), calls=%async_computation | async-start | bytes 5324800 | tf_op jit(solution)/shard_map/all_gather | solution.py:35
  9.4 185.5 %all-gather.11.cloned.1.call-start = ((), (), s32[]{:S(2)}) async-start(), calls=%async_computation.1 | async-start | bytes 15728640 | tf_op jit(solution)/shard_map/all_gather | solution.py:36
  165.4 0.8 copy-start.1
  165.4 1.5 copy-start.6
  165.4 2.4 copy-start
  165.4 3.0 copy-start.7
  165.4 3.3 copy-start.4
  165.4 176.3 %all-gather.13.cloned.1.call-start = ((), (), s32[]{:S(2)}) async-start(), calls=%async_computation.2 | async-start | bytes 2129920 | tf_op jit(solution)/shard_map/all_gather | solution.py:35
  196.5 4.2 %copy-start.5 = (bf16[64,512]{1,0:T(8,128)(2,1)S(1)}, bf16[64,512]{1,0:T(8,128)(2,1)}, u32[]{:S(2)}) copy-start(bf16[64,512]{1,0:T(8,128)(2,1)} %param.20) | copy-start | bytes 196612
  199.2 175.6 %all-gather.15.cloned.1.call-start = ((), (), s32[]{:S(2)}) async-start(), calls=%async_computation.3 | async-start | bytes 6291456 | tf_op jit(solution)/shard_map/all_gather | solution.py:36
  382.3 12.9 %copy-start.2 = (bf16[2,128,128]{2,1,0:T(8,128)(2,1)S(1)}, bf16[2,128,128]{2,1,0:T(8,128)(2,1)}, u32[]{:S(2)}) copy-start(bf16[2,128,128]{2,1,0:T(8,128)(2,1)} %param.22) | copy-start | bytes 196612
  382.3 12.9 %copy-start.3 = (bf16[2,128,128]{2,1,0:T(8,128)(2,1)S(1)}, bf16[2,128,128]{2,1,0:T(8,128)(2,1)}, u32[]{:S(2)}) copy-start(bf16[2,128,128]{2,1,0:T(8,128)(2,1)} %param.21) | copy-start | bytes 196612
Sparse Core Ops, SparseCore 0:
  10.9 154.3 all-gather.8
  167.5 27.2 all-gather.10
  199.3 142.3 all-gather.12
  343.6 20.0 all-gather.14

commit v2 on v1

--- a/solution.py
+++ b/solution.py
@@ -32,7 +32,10 @@
 
 
 def gather_rows(payload):
-    step = lax.all_gather(payload, ZY, axis=0, tiled=False)
+    step = lax.all_gather(payload, "y", axis=0, tiled=False)
+    step = lax.all_gather(step, "z", axis=0, tiled=False)
+    shape = step.shape
+    step = step.reshape((shape[0] * shape[1],) + shape[2:])
     return lax.all_gather(step, "core", axis=0, tiled=False)
 
 

time: 404 us -> 292 us (0.72)
  waiting for transfers between devices: 301 us -> 164 us
  blocking collectives: 13.8 us -> 40.4 us
    all_gather x2, waiting for transfers between devices: 290 us -> 149 us  [gather_rows(): step = lax.all_gather(step, 'z', axis=0, tiled=False)]
    all_gather x0 -> x2, blocking collectives: none -> 26.7 us  [gather_rows(): step = lax.all_gather(payload, 'y', axis=0, tiled=False)]
  transfers between devices with their start and end apart: 4 -> 4, of which waited for: 3 -> 3; matrix products, arithmetic and copies ran while one was open for 11% -> 16% of each run, Pallas kernels for 0% -> 0%
where the time goes in v2:
time: 292 us; the launch traced here: 291 us
  waiting for transfers between devices  164 us (56%)
  blocking collectives  40.4 us (14%)
  matrix products  38.1 us (13%)
  local copies, waits for them, and re-layouts  20 us (7%)
  between operations  14.1 us (5%)
  other arithmetic  13.8 us (5%)
    all_gather x2, waiting for transfers between devices, gather_rows(): step = lax.all_gather(step, 'z', axis=0, tiled=False)  149 us
    all_gather x2, blocking collectives, gather_rows(): step = lax.all_gather(payload, 'y', axis=0, tiled=False)  26.7 us
    dot_general x12, matrix products, attend(): jnp.einsum('thgk,khd->thgd', soft_weights.astype(jnp.bfloat16), values_sh...  19.3 us
    dot_general x12, matrix products, attend(): jnp.einsum('thgd,khd->thgk', q_local, keys_shaped, preferred_element_type...  15.4 us
    all_gather x2, waiting for transfers between devices, gather_rows(): return lax.all_gather(step, 'core', axis=0, tiled=False)  14.2 us
    all_gather x1, blocking collectives, body(): gathered = lax.all_gather(features, 'x', axis=1, tiled=True)  13.7 us
    reduce_sum x12, other arithmetic, attend(): new_sum = running_sum * factor + jnp.sum(soft_weights, axis=-1)  6.42 us
    slice x1, local copies, waits for them, and re-layouts, body(): cached_values = first[:, :, 2 * w_rows + old_rows:].reshape(-1, kv_width)  6.22 us
  transfers between devices with their start and end apart: 4, of which 3 were waited for; matrix products, arithmetic and copies ran while one was open for 16% of the time, Pallas kernels for 0%

profile of v2, /device:TPU:2, one launch (start us, length us, event | category | flops | bytes accessed | tf_op | source)
XLA Modules:
  0.0 290.8 jit_solution(1920048544598438604)
XLA Ops:
  8.7 13.6 %all-gather = bf16[1280,128]{1,0:T(8,128)(2,1)} all-gather(bf16[320,128]{1,0:T(8,128)(2,1)S(1)} %pad_maximum_fusion), channel_id=2, replica_groups=mesh['z'=16,'y'=4,'core'=2,'x'=4] {'y'}, dimensions={0}, use_global_device_ids=true | all-gather | bytes 409600 | tf_op jit(solution)/shard_map/all_gather | solution.py:35
  22.4 85.4 %all-gather.11.cloned.1.call-done = bf16[64,320,128]{2,1,0:T(8,128)(2,1)} async-done(((bf16[4,320,128]{2,1,0:T(8,128)(2,1)}), bf16[64,320,128]{2,1,0:T(8,128)(2,1)}) %all-gather.11.cloned.1.call-update) | async-done | bytes 5242896 | tf_op jit(solution)/shard_map/all_gather | solution.py:36
  110.0 13.7 %all_gather.38 = bf16[64,4096]{0,1:T(8,128)(2,1)S(1)} all-gather(bf16[64,1024]{0,1:T(8,128)(2,1)S(1)} %copy.62), channel_id=1, replica_groups=mesh['z'=16,'y'=4,'core'=2,'x'=4] {'x'}, dimensions={1}, use_global_device_ids=true | all-gather | bytes 655360 | tf_op jit(solution)/shard_map/all_gather | solution.py:82
  125.0 14.2 %all-gather.15.cloned.1.call-done = bf16[128,320,128]{2,1,0:T(8,128)(2,1)} async-done(((bf16[64,320,128]{2,1,0:T(8,128)(2,1)}), bf16[128,320,128]{2,1,0:T(8,128)(2,1)}) %all-gather.15.cloned.1.call-update) | async-done | bytes 10485776 | tf_op jit(solution)/shard_map/all_gather | solution.py:39
  139.2 1.7 fusion.41
  140.9 1.7 convolution_bitcast_fusion.3
  142.9 13.1 %all-gather.2 = bf16[256,256]{1,0:T(8,128)(2,1)} all-gather(bf16[64,256]{1,0:T(8,128)(2,1)S(1)} %pad_maximum_fusion.1), channel_id=4, replica_groups=mesh['z'=16,'y'=4,'core'=2,'x'=4] {'y'}, dimensions={0}, use_global_device_ids=true | all-gather | bytes 163840 | tf_op jit(solution)/shard_map/all_gather | solution.py:35
  159.8 6.2 %fusion.74 = (bf16[2,64,128,128]{3,2,1,0:T(8,128)(2,1)}, bf16[2,64,128,128]{3,2,1,0:T(8,128)(2,1)}) fusion(bf16[2,64,320,128]{3,2,1,0:T(8,128)(2,1)} %bitcast.222), kind=kLoop, calls=%fused_computation.174 | loop fusion | bytes 16777216 | tf_op jit(solution)/shard_map/slice | solution.py:80
  166.0 64.0 %all-gather.13.cloned.1.call-done = bf16[64,64,256]{2,1,0:T(8,128)(2,1)} async-done(((bf16[4,64,256]{2,1,0:T(8,128)(2,1)}), bf16[64,64,256]{2,1,0:T(8,128)(2,1)}) %all-gather.13.cloned.1.call-update) | async-done | bytes 2097168 | tf_op jit(solution)/shard_map/all_gather | solution.py:36
  230.0 33.0 %while.30 = (s32[]{:T(128)}, f32[64,1,4]{0,2,1:T(4,128)S(1)}, f32[64,1,4]{0,2,1:T(4,128)S(1)}, f32[64,1,4,128]{3,0,2,1:T(8,128)S(1)}, pred[8,2048]{1,0:T(8,128)(...) while((s32[]{:T(128)}, f32[64,1,4]{0,2,1:T(4,128)S(1)}, ...), condition=%wide.region_10.11_spmd.clone, body=%wide.region_7.0_spmd.clone.sunk | while | flops 273778176 | bytes 8264361 | solution.py:174
  230.3 1.6 fusion.96
  232.4 1.6 fusion.99
  234.4 1.6 fusion.96
  236.6 1.6 fusion.99
  238.5 1.6 fusion.96
  240.7 1.6 fusion.99
  242.6 1.6 fusion.96
  244.8 1.7 fusion.99
  246.8 1.7 fusion.96
  249.0 1.6 fusion.99
  251.0 1.6 fusion.96
  253.2 1.6 fusion.99
  255.1 1.6 fusion.96
  259.2 1.6 fusion.96
  261.4 1.6 fusion.99
  263.1 3.8 %fusion.75 = (bf16[8192,128]{1,0:T(8,128)(2,1)}, bf16[8192,128]{1,0:T(8,128)(2,1)S(1)}) fusion(bf16[8192,256]{1,0:T(8,128)(2,1)} %bitcast.223), kind=kLoop, calls=%fused_computation.175 | loop fusion | bytes 8388608 | tf_op jit(solution)/shard_map/slice | solution.py:197
  266.9 3.7 %gather_fusion = bf16[256,256]{1,0:T(8,128)(2,1)S(1)} fusion(bf16[8192,256]{1,0:T(8,128)(2,1)} %bitcast.224, s32[1024]{0:T(1024)S(1)} %pad_clamp_fusion), kind=kCustom, calls=%fused_computation.3 | custom fusion | bytes 263168 | tf_op jit(solution)/shard_map/jit(_take)/gather | solution.py:229
  270.6 12.0 %while.29 = (s32[]{:T(128)}, f32[64,1,4]{0,2,1:T(4,128)S(1)}, f32[64,1,4]{0,2,1:T(4,128)S(1)}, f32[64,1,4,128]{3,0,2,1:T(8,128)S(1)}, s32[4,2048]{1,0:T(4,128)S(...) while((s32[]{:T(128)}, f32[64,1,4]{0,2,1:T(4,128)S(1)}, ...), condition=%wide.region_15.16_spmd, body=%wide.region_12.15_spmd.sunk | while | flops 273613568 | bytes 8258185 | solution.py:174
  272.0 1.6 fusion.93
  274.9 1.6 fusion.93
  277.9 1.6 fusion.93
  280.9 1.6 fusion.93
  (179 shorter events, 24.2 us)
Async XLA Ops:
  7.2 100.6 %all-gather.11.cloned.1.call-start = ((), (), s32[]{:S(2)}) async-start(), calls=%async_computation | async-start | bytes 5570560 | tf_op jit(solution)/shard_map/all_gather | solution.py:36
  22.4 116.8 %all-gather.15.cloned.1.call-start = ((), (), s32[]{:S(2)}) async-start(), calls=%async_computation.2 | async-start | bytes 15728640 | tf_op jit(solution)/shard_map/all_gather | solution.py:39
  107.8 0.8 copy-start.1
  107.8 1.3 copy-start.7
  107.8 1.3 copy-start.4
  107.8 1.5 copy-start
  107.8 1.8 copy-start.6
  107.8 122.1 %all-gather.13.cloned.1.call-start = ((), (), s32[]{:S(2)}) async-start(), calls=%async_computation.1 | async-start | bytes 2228224 | tf_op jit(solution)/shard_map/all_gather | solution.py:36
  142.6 16.5 %copy-start.5 = (bf16[64,512]{1,0:T(8,128)(2,1)S(1)}, bf16[64,512]{1,0:T(8,128)(2,1)}, u32[]{:S(2)}) copy-start(bf16[64,512]{1,0:T(8,128)(2,1)} %param.20) | copy-start | bytes 196612
  156.0 107.1 %all-gather.17.cloned.1.call-start = ((), (), s32[]{:S(2)}) async-start(), calls=%async_computation.3 | async-start | bytes 6291456 | tf_op jit(solution)/shard_map/all_gather | solution.py:39
  270.6 12.9 %copy-start.2 = (bf16[2,128,128]{2,1,0:T(8,128)(2,1)S(1)}, bf16[2,128,128]{2,1,0:T(8,128)(2,1)}, u32[]{:S(2)}) copy-start(bf16[2,128,128]{2,1,0:T(8,128)(2,1)} %param.22) | copy-start | bytes 196612
  270.6 12.9 %copy-start.3 = (bf16[2,128,128]{2,1,0:T(8,128)(2,1)S(1)}, bf16[2,128,128]{2,1,0:T(8,128)(2,1)}, u32[]{:S(2)}) copy-start(bf16[2,128,128]{2,1,0:T(8,128)(2,1)} %param.21) | copy-start | bytes 196612
Sparse Core Ops, SparseCore 0:
  22.5 85.2 all-gather.10
  109.9 29.2 all-gather.14
  156.1 73.8 all-gather.12
  231.9 21.0 all-gather.16
